TPU v7x, 32 devices: a whole 2x2x4 slice. The times are simulated.
32 devices in a mesh: dp: 4 (over y, x), feat: 8 (over z, core).
Axes of the slice: x: 2, y: 2, z: 4, core: 2. Of those that a mesh axis runs over, the one named last changes fastest.
Arguments:
- sketches: bfloat16 [4, 256, 65536], P('dp', None, 'feat'), may hold values from -24 to 24
Outputs:
- merged: bfloat16 [4, 256, 65536], P('dp', None, 'feat')
All inputs are finite; a program needn't handle non-finite values.
Results may differ from a plain program's by a relative error of at most 0.001.
The roundings to bfloat16 on the way count: a program that leaves them out, or rounds other values in their place, can miss the bound.
Values may be sent and summed in bfloat16 or wider, within the bound.
No kernel may reach another device: no remote copies, remote signals or barrier semaphores. Data moves between devices by JAX's collectives and lax.ppermute only.
A program may use at most 128 MiB of HBM per device.

v0:
```python
import jax
import jax.numpy as jnp
from jax import lax
from jax.sharding import PartitionSpec as P

LEVELS = 2


def from_partner(block, axis, stride):
    count = lax.axis_size(axis)
    route = []
    for low in range(count):
        high = low | 1 << stride
        if high != low and high < count:
            route += [(low, high), (high, low)]
    return lax.ppermute(block, axis, route)


def solve_rows(gram, count):
    size = gram.shape[0]
    average = jnp.trace(gram) / size
    kernel = jnp.eye(size, dtype=jnp.float32) + gram / average
    factor = jnp.linalg.cholesky(kernel)
    target = jnp.eye(size, count, dtype=jnp.float32)
    middle = lax.linalg.triangular_solve(factor, target, left_side=True, lower=True)
    inverse = lax.linalg.triangular_solve(
        factor, middle, left_side=True, lower=True, transpose_a=True
    )
    return inverse.T.astype(jnp.bfloat16)


def per_device(sketches):
    current = sketches[0]
    count = current.shape[0]
    position = lax.axis_index("dp")
    for level in range(LEVELS):
        is_lower = position // 2**level % 2 == 0
        partner = from_partner(current, "dp", level)
        lower = jnp.where(is_lower, current, partner)
        upper = jnp.where(is_lower, partner, current)
        stacked = jnp.concatenate([lower, upper], axis=0)
        partial_gram = jnp.dot(stacked, stacked.T, preferred_element_type=jnp.float32)
        gram_total = lax.psum(partial_gram, "feat")
        weights = solve_rows(gram_total, count)
        update = jnp.dot(weights, stacked, preferred_element_type=jnp.float32)
        fresh = (lower.astype(jnp.float32) - update).astype(jnp.bfloat16)
        current = fresh
    return current[None]


def solution(mesh):
    placed = (P("dp", None, "feat"),)
    return jax.shard_map(
        per_device, mesh=mesh, in_specs=placed, out_specs=P("dp", None, "feat"), check_vma=False
    )
```

profile of v0, /device:TPU:0, one launch (start us, length us, event | category | flops | bytes accessed | tf_op | source)
XLA Modules:
  0.0 661.4 jit_solution(7594506524148744572)
XLA Ops:
  9.5 90.9 %collective-permute-done = bf16[256,8192]{1,0:T(8,128)(2,1)} collective-permute-done((bf16[256,8192]{1,0:T(8,128)(2,1)}, bf16[256,8192]{1,0:T(8,128)(2,1)}, u32[]{:S(2)}, u32[]{:S(2)}) %collective-permute-start) | collective-permute-done | bytes 4194336 | tf_op jit(solution)/shard_map/ppermute | solution.py:16
  107.4 9.1 %fusion.4 = f32[512,512]{0,1:T(8,128)} fusion(bf16[256,8192]{1,0:T(8,128)(2,1)S(1)} %get-tuple-element.62, bf16[256,8192]{1,0:T(8,128)(2,1)} %get-tuple-element.63), kind=kOutput, calls=%fused_computation.12 | convolution fusion | flops 4311744512 | bytes 9437184 | tf_op jit(solution)/shard_map/dot_general | solution.py:42
  117.1 60.3 %all-reduce.4.cloned.1.call-done = f32[512,512]{0,1:T(8,128)} async-done(((f32[512,512]{0,1:T(8,128)}), f32[512,512]{0,1:T(8,128)}) %all-reduce.4.cloned.1.call-update) | async-done | bytes 1048592 | tf_op jit(solution)/shard_map/psum | solution.py:43
  185.2 11.7 %cholesky.286 = f32[128,128]{1,0:T(8,128)S(1)} custom-call(f32[128,128]{1,0:T(8,128)S(1)} %cholesky.426), custom_call_target="Cholesky" | custom-call | tf_op jit(solution)/shard_map/jit(cholesky)/cholesky | solution.py:23
  197.1 9.8 %custom-call.31 = f32[1,128,128]{1,2,0:T(8,128)S(1)} custom-call(f32[1,128,128]{2,1,0:T(8,128)S(1)} %get-tuple-element.83), custom_call_target="InvertDiagBlocksLowerTriangular" | custom-call | tf_op jit(solution)/shard_map/jit(cholesky)/cholesky | solution.py:23
  209.4 11.7 %cholesky.305 = f32[128,128]{1,0:T(8,128)S(1)} custom-call(f32[128,128]{1,0:T(8,128)S(1)} %cholesky.430), custom_call_target="Cholesky" | custom-call | tf_op jit(solution)/shard_map/jit(cholesky)/cholesky | solution.py:23
  221.2 10.0 %custom-call.32 = f32[1,128,128]{1,2,0:T(8,128)S(1)} custom-call(f32[1,128,128]{2,1,0:T(8,128)S(1)} %get-tuple-element.80), custom_call_target="InvertDiagBlocksLowerTriangular" | custom-call | tf_op jit(solution)/shard_map/jit(cholesky)/cholesky | solution.py:23
  232.7 11.7 %cholesky.326 = f32[128,128]{1,0:T(8,128)S(1)} custom-call(f32[128,128]{1,0:T(8,128)S(1)} %cholesky.435), custom_call_target="Cholesky" | custom-call | tf_op jit(solution)/shard_map/jit(cholesky)/cholesky | solution.py:23
  245.1 9.8 %custom-call.33 = f32[1,128,128]{1,2,0:T(8,128)S(1)} custom-call(f32[1,128,128]{2,1,0:T(8,128)S(1)} %get-tuple-element.77), custom_call_target="InvertDiagBlocksLowerTriangular" | custom-call | tf_op jit(solution)/shard_map/jit(cholesky)/cholesky | solution.py:23
  256.4 11.9 %cholesky.343 = f32[128,128]{1,0:T(8,128)S(1)} custom-call(f32[128,128]{1,0:T(8,128)S(1)} %convolution_subtract_fusion.17), custom_call_target="Cholesky" | custom-call | tf_op jit(solution)/shard_map/jit(cholesky)/cholesky | solution.py:23
  280.6 39.3 %custom-call.35 = f32[4,128,128]{1,2,0:T(8,128)S(1)} custom-call(f32[4,128,128]{2,1,0:T(8,128)S(1)} %get-tuple-element.37), custom_call_target="InvertDiagBlocksLowerTriangular" | custom-call | tf_op jit(solution)/shard_map/triangular_solve/custom-call.8 | solution.py:26
  324.4 8.1 %subtract_convert_fusion.1 = bf16[256,8192]{1,0:T(8,128)(2,1)} fusion(bf16[256,8192]{1,0:T(8,128)(2,1)} %get-tuple-element.63, bf16[256,8192]{1,0:T(8,128)(2,1)S(1)} %copy-done.3, f32[128,256]{1,0:T(8,128)S(1)} %fusion.84, f32[128,256]{1,0:T(8,128)S(1)} %fusion.82, f32[128,256]{1,0:T(8,128)S(1)} %fusion.80, bf16[128,256]{1,0:T(8,128)(2,1)S(1)} %fusion.78), kind=kOutput, calls=%fused_computation.7 | convolution fusion | flops 2171600896 | bytes 13041664 | tf_op jit(solution)/shard_map/dot_general | solution.py:45
  334.0 89.4 %collective-permute-done.1 = bf16[256,8192]{1,0:T(8,128)(2,1)} collective-permute-done((bf16[256,8192]{1,0:T(8,128)(2,1)}, bf16[256,8192]{1,0:T(8,128)(2,1)}, u32[]{:S(2)}, u32[]{:S(2)}) %collective-permute-start.1) | collective-permute-done | bytes 4194336 | tf_op jit(solution)/shard_map/ppermute | solution.py:16
  430.9 9.0 %fusion.1 = f32[512,512]{0,1:T(8,128)} fusion(bf16[256,8192]{1,0:T(8,128)(2,1)} %get-tuple-element.61, bf16[256,8192]{1,0:T(8,128)(2,1)S(1)} %get-tuple-element.60), kind=kOutput, calls=%fused_computation.9 | convolution fusion | flops 4311744512 | bytes 9437184 | tf_op jit(solution)/shard_map/dot_general | solution.py:42
  440.0 59.3 %all-reduce.6.cloned.1.call-done = f32[512,512]{0,1:T(8,128)} async-done(((f32[512,512]{0,1:T(8,128)}), f32[512,512]{0,1:T(8,128)}) %all-reduce.6.cloned.1.call-update) | async-done | bytes 1048592 | tf_op jit(solution)/shard_map/psum | solution.py:43
  507.2 11.7 %cholesky.358 = f32[128,128]{1,0:T(8,128)S(1)} custom-call(f32[128,128]{1,0:T(8,128)S(1)} %cholesky.439), custom_call_target="Cholesky" | custom-call | tf_op jit(solution)/shard_map/jit(cholesky)/cholesky | solution.py:23
  519.1 9.8 %custom-call.36 = f32[1,128,128]{1,2,0:T(8,128)S(1)} custom-call(f32[1,128,128]{2,1,0:T(8,128)S(1)} %get-tuple-element.73), custom_call_target="InvertDiagBlocksLowerTriangular" | custom-call | tf_op jit(solution)/shard_map/jit(cholesky)/cholesky | solution.py:23
  531.4 11.9 %cholesky.377 = f32[128,128]{1,0:T(8,128)S(1)} custom-call(f32[128,128]{1,0:T(8,128)S(1)} %cholesky.443), custom_call_target="Cholesky" | custom-call | tf_op jit(solution)/shard_map/jit(cholesky)/cholesky | solution.py:23
  544.7 9.8 %custom-call.37 = f32[1,128,128]{1,2,0:T(8,128)S(1)} custom-call(f32[1,128,128]{2,1,0:T(8,128)S(1)} %get-tuple-element.70), custom_call_target="InvertDiagBlocksLowerTriangular" | custom-call | tf_op jit(solution)/shard_map/jit(cholesky)/cholesky | solution.py:23
  556.0 11.7 %cholesky.398 = f32[128,128]{1,0:T(8,128)S(1)} custom-call(f32[128,128]{1,0:T(8,128)S(1)} %cholesky.448), custom_call_target="Cholesky" | custom-call | tf_op jit(solution)/shard_map/jit(cholesky)/cholesky | solution.py:23
  568.5 9.8 %custom-call.38 = f32[1,128,128]{1,2,0:T(8,128)S(1)} custom-call(f32[1,128,128]{2,1,0:T(8,128)S(1)} %get-tuple-element.67), custom_call_target="InvertDiagBlocksLowerTriangular" | custom-call | tf_op jit(solution)/shard_map/jit(cholesky)/cholesky | solution.py:23
  579.9 11.7 %cholesky.415 = f32[128,128]{1,0:T(8,128)S(1)} custom-call(f32[128,128]{1,0:T(8,128)S(1)} %convolution_subtract_fusion.16), custom_call_target="Cholesky" | custom-call | tf_op jit(solution)/shard_map/jit(cholesky)/cholesky | solution.py:23
  595.1 8.1 %while.9 = (s32[]{:T(128)}, f32[512,512]{1,0:T(8,128)S(1)}, s32[4,2]{0,1:T(2,128)S(1)}, f32[4,128,128]{2,1,0:T(8,128)S(1)}, s32[]{:T(128)}) while((s32[]{:T(128)}, f32[512,512]{1,0:T(8,128)S(1)}, s32[4,2]{0,1:T(2,128)S(1)}, f32[4,128,128]{2,1,0:T(8,128)S(1)}, s32[]{:T(128)}) %tuple.71), condition=%wide.while_cond.1.clone, body=%wide.while_body.1.clone.sunk | while | flops 2 | bytes 131181 | solution.py:26
  603.3 39.6 %custom-call.40 = f32[4,128,128]{1,2,0:T(8,128)S(1)} custom-call(f32[4,128,128]{2,1,0:T(8,128)S(1)} %get-tuple-element.39), custom_call_target="InvertDiagBlocksLowerTriangular" | custom-call | tf_op jit(solution)/shard_map/triangular_solve/custom-call.8 | solution.py:26
  (128 shorter events, 90.6 us)
Async XLA Ops:
  6.5 170.9 %all-reduce.4.cloned.1.call-start = ((), (), s32[]{:S(2)}) async-start(), calls=%async_computation | async-start | bytes 2097152 | tf_op jit(solution)/shard_map/psum | solution.py:43
  6.5 93.9 %collective-permute-start = (bf16[256,8192]{1,0:T(8,128)(2,1)}, bf16[256,8192]{1,0:T(8,128)(2,1)}, u32[]{:S(2)}, u32[]{:S(2)}) collective-permute-start(bf16[256,8192]{1,0:T(8,128)(2,1)} %bitcast.133), channel_id=1, source_target_pairs={{0,8},{8,0},{16,24},{24,16},{1,9},{9,1},{17,25},{25,17},{2,10},{10... | collective-permute-start | bytes 12582920 | tf_op jit(solution)/shard_map/ppermute | solution.py:16
  105.5 1.9 copy-start.2
  116.5 382.7 %all-reduce.6.cloned.1.call-start = ((), (), s32[]{:S(2)}) async-start(), calls=%async_computation.1 | async-start | bytes 2097152 | tf_op jit(solution)/shard_map/psum | solution.py:43
  177.4 5.4 copy-start
  184.2 1.0 copy-start.7
  319.9 4.5 copy-start.3
  332.6 90.8 %collective-permute-start.1 = (bf16[256,8192]{1,0:T(8,128)(2,1)}, bf16[256,8192]{1,0:T(8,128)(2,1)}, u32[]{:S(2)}, u32[]{:S(2)}) collective-permute-start(bf16[256,8192]{1,0:T(8,128)(2,1)} %subtract_convert_fusion.1), channel_id=1, source_target_pairs={{0,16},{16,0},{8,24},{24,8},{1,17},{17,1},{9,25},{25,9},{2,18},{18... | collective-permute-start | bytes 12582920 | tf_op jit(solution)/shard_map/ppermute | solution.py:16
  428.9 2.0 copy-start.4
  499.2 5.5 copy-start.1
  506.2 1.0 copy-start.6
  642.9 4.5 copy-start.5
Sparse Core Ops, SparseCore 0:
  116.6 60.7 all-reduce.3
  440.1 59.1 all-reduce.5
where the time goes:
time: 666 us; the launch traced here: 661 us
  waiting for transfers between devices  300 us (45%)
  other arithmetic  258 us (39%)
  matrix products  53 us (8%)
  local copies, waits for them, and re-layouts  25.1 us (4%)
  between operations  20.7 us (3%)
    ppermute x2, waiting for transfers between devices, from_partner(): return lax.ppermute(block, axis, route)  180 us
    another operation x29, other arithmetic, solve_rows(): factor = jnp.linalg.cholesky(kernel)  158 us
    psum x2, waiting for transfers between devices, per_device(): gram_total = lax.psum(partial_gram, 'feat')  120 us
    another operation x5, other arithmetic, solve_rows(): lax.linalg.triangular_solve(factor, middle, left_side=True, lower=True, t...  79.1 us
    dot_general x2, matrix products, per_device(): jnp.dot(stacked, stacked.T, preferred_element_type=jnp.float32)  18.1 us
    another operation x27, local copies, waits for them, and re-layouts, solve_rows(): lax.linalg.triangular_solve(factor, middle, left_side=True, lower=True, t...  16.1 us
    dot_general x2, matrix products, per_device(): update = jnp.dot(weights, stacked, preferred_element_type=jnp.float32)  15 us
  transfers between devices with their start and end apart: 4, of which 4 were waited for; matrix products, arithmetic and copies ran while one was open for 0% of the time, Pallas kernels for 0%

commit v1 on v0

--- a/solution.py
+++ b/solution.py
@@ -40,7 +40,11 @@
         upper = jnp.where(is_lower, partner, current)
         stacked = jnp.concatenate([lower, upper], axis=0)
         partial_gram = jnp.dot(stacked, stacked.T, preferred_element_type=jnp.float32)
-        gram_total = lax.psum(partial_gram, "feat")
+        gram_total = partial_gram
+        for hop in (1, 2, 4):
+            gram_total = gram_total + lax.ppermute(
+                gram_total, "feat", [(dev, dev ^ hop) for dev in range(8)]
+            )
         weights = solve_rows(gram_total, count)
         update = jnp.dot(weights, stacked, preferred_element_type=jnp.float32)
         fresh = (lower.astype(jnp.float32) - update).astype(jnp.bfloat16)

time: 666 us -> 699 us (1.050)
  waiting for transfers between devices: 300 us -> 324 us
  between operations: 20.7 us -> 7.5 us
  starting transfers between devices: 4.95 us -> 14.5 us
  other arithmetic: 258 us -> 267 us
    ppermute x0 -> x6, waiting for transfers between devices: none -> 143 us  [per_device(): lax.ppermute(gram_total, 'feat', [(dev, dev ^ hop) for dev in range(8)])]
    psum x2 -> x0, waiting for transfers between devices: 120 us -> none  [per_device(): gram_total = lax.psum(partial_gram, 'feat')]
    ppermute x0 -> x6, starting transfers between devices: none -> 9.99 us  [per_device(): lax.ppermute(gram_total, 'feat', [(dev, dev ^ hop) for dev in range(8)])]
    another operation x29, other arithmetic: 158 us -> 168 us  [solve_rows(): factor = jnp.linalg.cholesky(kernel)]
  transfers between devices with their start and end apart: 4 -> 8, of which waited for: 4 -> 8; matrix products, arithmetic and copies ran while one was open for 0% -> 0% of each run, Pallas kernels for 0% -> 0%
where the time goes in v1:
time: 699 us; the launch traced here: 690 us
  waiting for transfers between devices  324 us (46%)
  other arithmetic  267 us (38%)
  matrix products  55.9 us (8%)
  local copies, waits for them, and re-layouts  20.7 us (3%)
  starting transfers between devices  14.5 us (2%)
  between operations  7.5 us (1%)
    ppermute x2, waiting for transfers between devices, from_partner(): return lax.ppermute(block, axis, route)  181 us
    another operation x29, other arithmetic, solve_rows(): factor = jnp.linalg.cholesky(kernel)  168 us
    ppermute x6, waiting for transfers between devices, per_device(): lax.ppermute(gram_total, 'feat', [(dev, dev ^ hop) for dev in range(8)])  143 us
    another operation x5, other arithmetic, solve_rows(): lax.linalg.triangular_solve(factor, middle, left_side=True, lower=True, t...  79.1 us
    dot_general x2, matrix products, per_device(): jnp.dot(stacked, stacked.T, preferred_element_type=jnp.float32)  21 us
    another operation x27, local copies, waits for them, and re-layouts, solve_rows(): lax.linalg.triangular_solve(factor, middle, left_side=True, lower=True, t...  15.8 us
    dot_general x2, matrix products, per_device(): update = jnp.dot(weights, stacked, preferred_element_type=jnp.float32)  15 us
  transfers between devices with their start and end apart: 8, of which 8 were waited for; matrix products, arithmetic and copies ran while one was open for 0% of the time, Pallas kernels for 0%

profile of v1, /device:TPU:0, one launch (start us, length us, event | category | flops | bytes accessed | tf_op | source)
XLA Modules:
  0.0 689.7 jit_solution(15332466483529554168)
XLA Ops:
  3.0 90.9 %collective-permute-done = bf16[256,8192]{1,0:T(8,128)(2,1)} collective-permute-done((bf16[256,8192]{1,0:T(8,128)(2,1)}, bf16[256,8192]{1,0:T(8,128)(2,1)}, u32[]{:S(2)}, u32[]{:S(2)}) %collective-permute-start) | collective-permute-done | bytes 4194336 | tf_op jit(solution)/shard_map/ppermute | solution.py:16
  98.9 10.5 %fusion.4 = f32[512,512]{0,1:T(8,128)} fusion(bf16[256,8192]{1,0:T(8,128)(2,1)S(1)} %get-tuple-element.66, bf16[256,8192]{1,0:T(8,128)(2,1)} %get-tuple-element.67), kind=kOutput, calls=%fused_computation.12 | convolution fusion | flops 4311744512 | bytes 9437184 | tf_op jit(solution)/shard_map/dot_general | solution.py:42
  115.7 23.5 %collective-permute-done.2 = f32[512,512]{0,1:T(8,128)S(1)} collective-permute-done((f32[512,512]{0,1:T(8,128)S(1)}, f32[512,512]{0,1:T(8,128)S(1)}, u32[]{:S(2)}, u32[]{:S(2)}) %collective-permute-start.2) | collective-permute-done | bytes 1048608 | tf_op jit(solution)/shard_map/ppermute | solution.py:45
  142.2 45.1 %collective-permute-done.3 = f32[512,512]{0,1:T(8,128)} collective-permute-done((f32[512,512]{0,1:T(8,128)S(1)}, f32[512,512]{0,1:T(8,128)}, u32[]{:S(2)}, u32[]{:S(2)}) %collective-permute-start.3) | collective-permute-done | bytes 1048608 | tf_op jit(solution)/shard_map/ppermute | solution.py:45
  193.9 11.7 %cholesky.286 = f32[128,128]{1,0:T(8,128)S(1)} custom-call(f32[128,128]{1,0:T(8,128)S(1)} %cholesky.426), custom_call_target="Cholesky" | custom-call | tf_op jit(solution)/shard_map/jit(cholesky)/cholesky | solution.py:23
  205.8 9.8 %custom-call.31 = f32[1,128,128]{1,2,0:T(8,128)S(1)} custom-call(f32[1,128,128]{2,1,0:T(8,128)S(1)} %get-tuple-element.87), custom_call_target="InvertDiagBlocksLowerTriangular" | custom-call | tf_op jit(solution)/shard_map/jit(cholesky)/cholesky | solution.py:23
  218.1 12.0 %cholesky.305 = f32[128,128]{1,0:T(8,128)S(1)} custom-call(f32[128,128]{1,0:T(8,128)S(1)} %cholesky.430), custom_call_target="Cholesky" | custom-call | tf_op jit(solution)/shard_map/jit(cholesky)/cholesky | solution.py:23
  230.1 9.8 %custom-call.32 = f32[1,128,128]{1,2,0:T(8,128)S(1)} custom-call(f32[1,128,128]{2,1,0:T(8,128)S(1)} %get-tuple-element.84), custom_call_target="InvertDiagBlocksLowerTriangular" | custom-call | tf_op jit(solution)/shard_map/jit(cholesky)/cholesky | solution.py:23
  241.5 11.7 %cholesky.326 = f32[128,128]{1,0:T(8,128)S(1)} custom-call(f32[128,128]{1,0:T(8,128)S(1)} %cholesky.435), custom_call_target="Cholesky" | custom-call | tf_op jit(solution)/shard_map/jit(cholesky)/cholesky | solution.py:23
  254.0 19.3 %custom-call.33 = f32[1,128,128]{1,2,0:T(8,128)S(1)} custom-call(f32[1,128,128]{2,1,0:T(8,128)S(1)} %get-tuple-element.81), custom_call_target="InvertDiagBlocksLowerTriangular" | custom-call | tf_op jit(solution)/shard_map/jit(cholesky)/cholesky | solution.py:23
  274.7 11.7 %cholesky.343 = f32[128,128]{1,0:T(8,128)S(1)} custom-call(f32[128,128]{1,0:T(8,128)S(1)} %convolution_subtract_fusion.17), custom_call_target="Cholesky" | custom-call | tf_op jit(solution)/shard_map/jit(cholesky)/cholesky | solution.py:23
  298.4 39.3 %custom-call.35 = f32[4,128,128]{1,2,0:T(8,128)S(1)} custom-call(f32[4,128,128]{2,1,0:T(8,128)S(1)} %get-tuple-element.37), custom_call_target="InvertDiagBlocksLowerTriangular" | custom-call | tf_op jit(solution)/shard_map/triangular_solve/custom-call.8 | solution.py:26
  352.0 90.2 %collective-permute-done.4 = bf16[256,8192]{1,0:T(8,128)(2,1)} collective-permute-done((bf16[256,8192]{1,0:T(8,128)(2,1)}, bf16[256,8192]{1,0:T(8,128)(2,1)}, u32[]{:S(2)}, u32[]{:S(2)}) %collective-permute-start.4) | collective-permute-done | bytes 4194336 | tf_op jit(solution)/shard_map/ppermute | solution.py:16
  447.6 10.5 %fusion.1 = f32[512,512]{0,1:T(8,128)} fusion(bf16[256,8192]{1,0:T(8,128)(2,1)} %get-tuple-element.65, bf16[256,8192]{1,0:T(8,128)(2,1)S(1)} %get-tuple-element.64), kind=kOutput, calls=%fused_computation.9 | convolution fusion | flops 4311744512 | bytes 9437184 | tf_op jit(solution)/shard_map/dot_general | solution.py:42
  464.2 23.5 %collective-permute-done.6 = f32[512,512]{0,1:T(8,128)S(1)} collective-permute-done((f32[512,512]{0,1:T(8,128)S(1)}, f32[512,512]{0,1:T(8,128)S(1)}, u32[]{:S(2)}, u32[]{:S(2)}) %collective-permute-start.6) | collective-permute-done | bytes 1048608 | tf_op jit(solution)/shard_map/ppermute | solution.py:45
  491.4 45.4 %collective-permute-done.7 = f32[512,512]{0,1:T(8,128)S(1)} collective-permute-done((f32[512,512]{0,1:T(8,128)S(1)}, f32[512,512]{0,1:T(8,128)S(1)}, u32[]{:S(2)}, u32[]{:S(2)}) %collective-permute-start.7) | collective-permute-done | bytes 1048608 | tf_op jit(solution)/shard_map/ppermute | solution.py:45
  542.2 11.7 %cholesky.358 = f32[128,128]{1,0:T(8,128)S(1)} custom-call(f32[128,128]{1,0:T(8,128)S(1)} %cholesky.439), custom_call_target="Cholesky" | custom-call | tf_op jit(solution)/shard_map/jit(cholesky)/cholesky | solution.py:23
  554.1 9.8 %custom-call.36 = f32[1,128,128]{1,2,0:T(8,128)S(1)} custom-call(f32[1,128,128]{2,1,0:T(8,128)S(1)} %get-tuple-element.77), custom_call_target="InvertDiagBlocksLowerTriangular" | custom-call | tf_op jit(solution)/shard_map/jit(cholesky)/cholesky | solution.py:23
  566.6 11.7 %cholesky.377 = f32[128,128]{1,0:T(8,128)S(1)} custom-call(f32[128,128]{1,0:T(8,128)S(1)} %cholesky.443), custom_call_target="Cholesky" | custom-call | tf_op jit(solution)/shard_map/jit(cholesky)/cholesky | solution.py:23
  579.7 9.8 %custom-call.37 = f32[1,128,128]{1,2,0:T(8,128)S(1)} custom-call(f32[1,128,128]{2,1,0:T(8,128)S(1)} %get-tuple-element.74), custom_call_target="InvertDiagBlocksLowerTriangular" | custom-call | tf_op jit(solution)/shard_map/jit(cholesky)/cholesky | solution.py:23
  591.1 11.7 %cholesky.398 = f32[128,128]{1,0:T(8,128)S(1)} custom-call(f32[128,128]{1,0:T(8,128)S(1)} %cholesky.448), custom_call_target="Cholesky" | custom-call | tf_op jit(solution)/shard_map/jit(cholesky)/cholesky | solution.py:23
  603.5 10.0 %custom-call.38 = f32[1,128,128]{1,2,0:T(8,128)S(1)} custom-call(f32[1,128,128]{2,1,0:T(8,128)S(1)} %get-tuple-element.71), custom_call_target="InvertDiagBlocksLowerTriangular" | custom-call | tf_op jit(solution)/shard_map/jit(cholesky)/cholesky | solution.py:23
  615.0 11.7 %cholesky.415 = f32[128,128]{1,0:T(8,128)S(1)} custom-call(f32[128,128]{1,0:T(8,128)S(1)} %convolution_subtract_fusion.16), custom_call_target="Cholesky" | custom-call | tf_op jit(solution)/shard_map/jit(cholesky)/cholesky | solution.py:23
  638.3 39.6 %custom-call.40 = f32[4,128,128]{1,2,0:T(8,128)S(1)} custom-call(f32[4,128,128]{2,1,0:T(8,128)S(1)} %get-tuple-element.39), custom_call_target="InvertDiagBlocksLowerTriangular" | custom-call | tf_op jit(solution)/shard_map/triangular_solve/custom-call.8 | solution.py:26
  (134 shorter events, 117.2 us)
Async XLA Ops:
  0.0 93.9 %collective-permute-start = (bf16[256,8192]{1,0:T(8,128)(2,1)}, bf16[256,8192]{1,0:T(8,128)(2,1)}, u32[]{:S(2)}, u32[]{:S(2)}) collective-permute-start(bf16[256,8192]{1,0:T(8,128)(2,1)} %bitcast.133), channel_id=1, source_target_pairs={{0,8},{8,0},{16,24},{24,16},{1,9},{9,1},{17,25},{25,17},{2,10},{10... | collective-permute-start | bytes 12582920 | tf_op jit(solution)/shard_map/ppermute | solution.py:16
  98.9 10.5 %copy-start = (bf16[256,8192]{1,0:T(8,128)(2,1)}, bf16[256,8192]{1,0:T(8,128)(2,1)S(1)}, u32[]{:S(2)}) copy-start(bf16[256,8192]{1,0:T(8,128)(2,1)S(1)} %get-tuple-element.66) | copy-start | bytes 12582916
  109.5 2.9 collective-permute-start.1
  113.8 25.4 %collective-permute-start.2 = (f32[512,512]{0,1:T(8,128)S(1)}, f32[512,512]{0,1:T(8,128)S(1)}, u32[]{:S(2)}, u32[]{:S(2)}) collective-permute-start(f32[512,512]{0,1:T(8,128)S(1)} %add.67), channel_id=1, source_target_pairs={{0,2},{1,3},{2,0},{3,1},{4,6},{5,7},{6,4},{7,5},{8,10},{9,11},{10,... | collective-permute-start | bytes 3145736 | tf_op jit(solution)/shard_map/ppermute | solution.py:45
  139.3 48.0 %collective-permute-start.3 = (f32[512,512]{0,1:T(8,128)S(1)}, f32[512,512]{0,1:T(8,128)}, u32[]{:S(2)}, u32[]{:S(2)}) collective-permute-start(f32[512,512]{0,1:T(8,128)S(1)} %add.68), channel_id=1, source_target_pairs={{0,4},{1,5},{2,6},{3,7},{4,0},{5,1},{6,2},{7,3},{8,12},{9,13},{10,... | collective-permute-start | bytes 3145736 | tf_op jit(solution)/shard_map/ppermute | solution.py:45
  192.9 1.0 copy-start.5
  337.7 4.5 copy-start.1
  350.4 91.7 %collective-permute-start.4 = (bf16[256,8192]{1,0:T(8,128)(2,1)}, bf16[256,8192]{1,0:T(8,128)(2,1)}, u32[]{:S(2)}, u32[]{:S(2)}) collective-permute-start(bf16[256,8192]{1,0:T(8,128)(2,1)} %subtract_convert_fusion.1), channel_id=1, source_target_pairs={{0,16},{16,0},{8,24},{24,8},{1,17},{17,1},{9,25},{25,9},{2,18},{18... | collective-permute-start | bytes 12582920 | tf_op jit(solution)/shard_map/ppermute | solution.py:16
  447.6 10.5 %copy-start.2 = (bf16[256,8192]{1,0:T(8,128)(2,1)}, bf16[256,8192]{1,0:T(8,128)(2,1)S(1)}, u32[]{:S(2)}) copy-start(bf16[256,8192]{1,0:T(8,128)(2,1)S(1)} %get-tuple-element.64) | copy-start | bytes 12582916
  458.1 2.9 collective-permute-start.5
  462.4 25.3 %collective-permute-start.6 = (f32[512,512]{0,1:T(8,128)S(1)}, f32[512,512]{0,1:T(8,128)S(1)}, u32[]{:S(2)}, u32[]{:S(2)}) collective-permute-start(f32[512,512]{0,1:T(8,128)S(1)} %add.71), channel_id=1, source_target_pairs={{0,2},{1,3},{2,0},{3,1},{4,6},{5,7},{6,4},{7,5},{8,10},{9,11},{10,... | collective-permute-start | bytes 3145736 | tf_op jit(solution)/shard_map/ppermute | solution.py:45
  487.9 48.9 %collective-permute-start.7 = (f32[512,512]{0,1:T(8,128)S(1)}, f32[512,512]{0,1:T(8,128)S(1)}, u32[]{:S(2)}, u32[]{:S(2)}) collective-permute-start(f32[512,512]{0,1:T(8,128)S(1)} %add.72), channel_id=1, source_target_pairs={{0,4},{1,5},{2,6},{3,7},{4,0},{5,1},{6,2},{7,3},{8,12},{9,13},{10,... | collective-permute-start | bytes 3145736 | tf_op jit(solution)/shard_map/ppermute | solution.py:45
  541.2 1.0 copy-start.4
  677.9 4.5 copy-start.3
